TPU v7x, 512 devices: a whole 4x4x16 slice. The times are simulated.
512 devices in a mesh: wide: 32 (over z, core), narrow: 16 (over y, x).
Axes of the slice: x: 4, y: 4, z: 16, core: 2. Of those that a mesh axis runs over, the one named last changes fastest.
Arguments:
- hidden: bfloat16 [2048, 2048], P('wide'), may hold values from -6 to 6
- attn_gain: float32 [2048], replicated, may hold values from 0.1 to 1.9
- expert_gain: float32 [2048], replicated, may hold values from 0.1 to 1.9
- query_weight: bfloat16 [2048, 2048], P('wide', 'narrow'), may hold values from -0.125 to 0.125
- key_weight: bfloat16 [2048, 2048], P('wide', 'narrow'), may hold values from -0.125 to 0.125
- value_weight: bfloat16 [2048, 2048], P('wide', 'narrow'), may hold values from -0.125 to 0.125
- output_weight: bfloat16 [2048, 2048], P('wide', 'narrow'), may hold values from -0.125 to 0.125
- router_weight: bfloat16 [2048, 64], replicated, may hold values from -0.125 to 0.125
- gate_weight: bfloat16 [64, 2048, 1024], P('wide', None, 'narrow'), may hold values from -0.125 to 0.125
- up_weight: bfloat16 [64, 2048, 1024], P('wide', None, 'narrow'), may hold values from -0.125 to 0.125
- down_weight: bfloat16 [64, 1024, 2048], P('wide', 'narrow'), may hold values from -0.1875 to 0.1875
- prefix_keys: bfloat16 [256, 8, 2048], P('wide', None, 'narrow'), may hold values from -6 to 6
- prefix_values: bfloat16 [256, 8, 2048], P('wide', None, 'narrow'), may hold values from -6 to 6
- cache_keys: bfloat16 [32, 1024, 2048], P('wide', None, 'narrow'), may hold values from -256 to 256
- cache_values: bfloat16 [32, 1024, 2048], P('wide', None, 'narrow'), may hold values from -6 to 6
- parents: int32 [32, 64], P('wide'), may hold values from 0 to 62, as said below
- cache_lengths: int32 [32], P('wide'), may hold values from 1 to 960, 15360 in all
- group_ids: int32 [32], replicated, may hold values from 0 to 7
- expert_ids: int32 [2048, 8], P('wide'), may hold values from 0 to 63, all different within a row; in each aligned block of 64 rows (0 to 63, 64 to 127, ...) at most 9 rows name the same one
- accepted: int32 [32], P('wide'), may hold values from 0 to 63
Outputs:
- layer_out: bfloat16 [2048, 2048], P('wide', 'narrow')
- new_keys: bfloat16 [32, 1024, 2048], P('wide', None, 'narrow')
- new_values: bfloat16 [32, 1024, 2048], P('wide', None, 'narrow')
Inputs may be any that keep to these rules, and one draw needn't show every extreme that they name: `parents`: node 0 of each tree is the root and its own parent; node i > 0 has its parent among nodes max(0, i - 4) to i - 1; the parent of node 63 is node 62. `expert_ids`: the 8 experts of a token differ; among the tokens of one index of wide no expert is named more than 9 times, a bound that some block reaches in some of them.
All inputs are finite; a program needn't handle non-finite values. No bound on the sum of `cache_lengths` on one device may be relied on, other than what follows from the above.
Results may differ from a plain program's by a relative error of at most 0.01.
The roundings to bfloat16 on the way count: a program that leaves them out, or rounds other values in their place, can miss the bound.
Values may be sent and summed in bfloat16 or wider, within the bound.
A program may use at most 64 MiB of HBM per device.

v0:
```python
import math
import jax
import jax.numpy as jnp
from jax import lax
from jax.sharding import PartitionSpec as P

HD = 128
E = 64
SINK = 4
WIN = 512
CAP = 9
norm_eps = 1e-06


def rms_scale(rows, row_gain):
    widened = rows.astype(jnp.float32)
    power_mean = jnp.mean(widened * widened, axis=-1, keepdims=True)
    return (widened * lax.rsqrt(power_mean + norm_eps) * row_gain).astype(jnp.bfloat16)


def tree_links(parents):
    tree_size = parents.shape[-1]
    node_ids = jnp.arange(tree_size, dtype=jnp.int32)
    linked = (node_ids[:, None] == node_ids[None, :]) | (parents[..., :, None] == node_ids)
    jumper = parents
    for doubling in range(tree_size.bit_length()):
        hop_table = (jumper[..., :, None] == node_ids).astype(jnp.float32)
        through = jnp.einsum(
            "...ij,...jk->...ik",
            hop_table,
            linked.astype(jnp.float32),
            precision=lax.Precision.HIGHEST,
        )
        linked = linked | (through > 0.5)
        jumper = jnp.take_along_axis(jumper, jumper, axis=-1)
    depths = jnp.sum(linked.astype(jnp.int32), axis=-1) - 1
    return (linked, depths)


def body(
    hidden,
    attn_gain,
    expert_gain,
    query_weight,
    key_weight,
    value_weight,
    output_weight,
    router_weight,
    gate_weight,
    up_weight,
    down_weight,
    prefix_keys,
    prefix_values,
    cache_keys,
    cache_values,
    parents,
    cache_lengths,
    group_ids,
    expert_ids,
    accepted,
):
    tok_count, model_width = hidden.shape
    req_count, tree_size = parents.shape
    cache_size = cache_keys.shape[1]
    local_width = query_weight.shape[1]
    head_size = HD
    head_count = local_width // head_size
    group_count = prefix_keys.shape[1]
    narrow_count = lax.axis_size("narrow")
    wide_count = lax.axis_size("wide")
    slice_width = model_width // narrow_count
    narrow_pos = lax.axis_index("narrow")
    wide_pos = lax.axis_index("wide")
    scale_factor = 1.0 / math.sqrt(head_size)
    normed = rms_scale(hidden, attn_gain)
    own_groups = lax.dynamic_slice_in_dim(group_ids, wide_pos * req_count, req_count)
    gathered = (
        lax.all_gather(query_weight, "wide", axis=0, tiled=True),
        lax.all_gather(key_weight, "wide", axis=0, tiled=True),
        lax.all_gather(value_weight, "wide", axis=0, tiled=True),
        lax.all_gather(output_weight, "wide", axis=0, tiled=True),
        lax.all_gather(prefix_keys, "wide", axis=0, tiled=True),
        lax.all_gather(prefix_values, "wide", axis=0, tiled=True),
    )
    query_full, key_full, value_full, output_full, shared_keys, shared_values = gathered
    prefix_len = shared_keys.shape[0]
    group_keys = jnp.take(
        shared_keys.reshape(prefix_len, group_count, head_count, head_size), own_groups, axis=1
    )
    group_values = jnp.take(
        shared_values.reshape(prefix_len, group_count, head_count, head_size), own_groups, axis=1
    )
    queries = jnp.dot(normed, query_full, preferred_element_type=jnp.float32).astype(jnp.bfloat16)
    keys_new = jnp.dot(normed, key_full, preferred_element_type=jnp.float32).astype(jnp.bfloat16)
    values_new = jnp.dot(normed, value_full, preferred_element_type=jnp.float32).astype(
        jnp.bfloat16
    )
    block_shape = (req_count, tree_size, head_count, head_size)
    query_blocks = queries.reshape(block_shape)
    key_blocks = keys_new.reshape(block_shape)
    value_blocks = values_new.reshape(block_shape)
    own_keys = cache_keys.reshape(req_count, cache_size, head_count, head_size)
    own_values = cache_values.reshape(req_count, cache_size, head_count, head_size)
    slot_ids = jnp.arange(cache_size, dtype=jnp.int32)
    lengths = cache_lengths[:, None]
    cache_mask = (slot_ids < lengths) & ((slot_ids < SINK) | (slot_ids >= lengths - WIN))
    ancestry, depths = tree_links(parents)
    cache_allowed = cache_mask[:, None, None, :]
    tree_allowed = ancestry[:, None, :, :]
    prefix_scores = (
        jnp.einsum("rqhd,prhd->rhqp", query_blocks, group_keys, preferred_element_type=jnp.float32)
        * scale_factor
    )
    cache_scores = (
        jnp.einsum("rqhd,rkhd->rhqk", query_blocks, own_keys, preferred_element_type=jnp.float32)
        * scale_factor
    )
    tree_scores = (
        jnp.einsum("rqhd,rkhd->rhqk", query_blocks, key_blocks, preferred_element_type=jnp.float32)
        * scale_factor
    )
    row_top = jnp.maximum(
        jnp.max(prefix_scores, axis=-1),
        jnp.maximum(
            jnp.max(jnp.where(cache_allowed, cache_scores, -jnp.inf), axis=-1),
            jnp.max(jnp.where(tree_allowed, tree_scores, -jnp.inf), axis=-1),
        ),
    )[..., None]
    prefix_weights = jnp.exp(prefix_scores - row_top)
    cache_weights = jnp.where(cache_allowed, jnp.exp(cache_scores - row_top), 0.0)
    tree_weights = jnp.where(tree_allowed, jnp.exp(tree_scores - row_top), 0.0)
    row_total = (
        jnp.sum(prefix_weights, axis=-1)
        + jnp.sum(cache_weights, axis=-1)
        + jnp.sum(tree_weights, axis=-1)
    )
    weighted = jnp.einsum(
        "rhqp,prhd->rqhd",
        prefix_weights.astype(jnp.bfloat16),
        group_values,
        preferred_element_type=jnp.float32,
    )
    weighted = weighted + jnp.einsum(
        "rhqk,rkhd->rqhd",
        cache_weights.astype(jnp.bfloat16),
        own_values,
        preferred_element_type=jnp.float32,
    )
    weighted = weighted + jnp.einsum(
        "rhqk,rkhd->rqhd",
        tree_weights.astype(jnp.bfloat16),
        value_blocks,
        preferred_element_type=jnp.float32,
    )
    attended = (
        (weighted / jnp.transpose(row_total, (0, 2, 1))[..., None])
        .astype(jnp.bfloat16)
        .reshape(tok_count, local_width)
    )
    partial_value = lax.dot_general(
        attended, output_full, (((1,), (1,)), ((), ())), preferred_element_type=jnp.float32
    )
    summed = lax.psum(partial_value, "narrow")
    mixed = (hidden.astype(jnp.float32) + summed).astype(jnp.bfloat16)
    mixed_part = lax.dynamic_slice_in_dim(mixed, narrow_pos * slice_width, slice_width, 1)
    normed_moe = rms_scale(mixed, expert_gain)
    logits = jnp.dot(normed_moe, router_weight, preferred_element_type=jnp.float32)
    expert_range = jnp.arange(E, dtype=jnp.int32)
    top_count = expert_ids.shape[1]
    matches = expert_ids[:, :, None] == expert_range
    chosen = jnp.sum(jnp.where(matches, logits[:, None, :], 0.0), axis=-1)
    shares = jax.nn.softmax(chosen, axis=-1)
    flat_experts = expert_ids.reshape(-1)
    expert_table = (flat_experts[:, None] == expert_range).astype(jnp.int32)
    earlier = jnp.cumsum(expert_table, axis=0) - expert_table
    slot_ranks = jnp.sum(earlier * expert_table, axis=1)
    targets = flat_experts * CAP + slot_ranks
    repeated = jnp.broadcast_to(
        normed_moe[:, None, :], (tok_count, top_count, model_width)
    ).reshape(tok_count * top_count, model_width)
    exp_local = gate_weight.shape[0]
    send_rows = jnp.zeros((E * CAP, model_width), jnp.bfloat16).at[targets].set(repeated)
    send_rows = send_rows.reshape(wide_count, exp_local, CAP, model_width)
    routed = lax.all_to_all(send_rows, "wide", split_axis=0, concat_axis=0, tiled=True)
    gate_out = jnp.einsum("secd,edf->secf", routed, gate_weight, preferred_element_type=jnp.float32)
    up_out = jnp.einsum("secd,edf->secf", routed, up_weight, preferred_element_type=jnp.float32)
    activated = (jax.nn.silu(gate_out) * up_out).astype(jnp.bfloat16)
    produced = jnp.einsum(
        "secf,efd->secd", activated, down_weight, preferred_element_type=jnp.float32
    ).astype(jnp.bfloat16)
    returned = lax.all_to_all(produced, "wide", split_axis=0, concat_axis=0, tiled=True)
    fetched = returned.reshape(E * CAP, model_width)[targets].reshape(
        tok_count, top_count, model_width
    )
    partial_moe = jnp.sum(shares[:, :, None] * fetched.astype(jnp.float32), axis=1)
    moe_part = lax.psum_scatter(partial_moe, "narrow", scatter_dimension=1, tiled=True)
    layer_out = (mixed_part.astype(jnp.float32) + moe_part).astype(jnp.bfloat16)
    on_path = jnp.take_along_axis(ancestry, accepted[:, None, None], axis=1)[:, 0, :]
    slots = jnp.where(on_path, cache_lengths[:, None] + depths, cache_size)
    request_rows = jnp.broadcast_to(
        jnp.arange(req_count, dtype=jnp.int32)[:, None], (req_count, tree_size)
    )
    new_keys = cache_keys.at[request_rows, slots].set(
        keys_new.reshape(req_count, tree_size, local_width), mode="drop"
    )
    new_values = cache_values.at[request_rows, slots].set(
        values_new.reshape(req_count, tree_size, local_width), mode="drop"
    )
    return (layer_out, new_keys, new_values)


def solution(mesh):
    in_specs = (
        P("wide", None),
        P(),
        P(),
        P("wide", "narrow"),
        P("wide", "narrow"),
        P("wide", "narrow"),
        P("wide", "narrow"),
        P(),
        P("wide", None, "narrow"),
        P("wide", None, "narrow"),
        P("wide", "narrow", None),
        P("wide", None, "narrow"),
        P("wide", None, "narrow"),
        P("wide", None, "narrow"),
        P("wide", None, "narrow"),
        P("wide", None),
        P("wide"),
        P(),
        P("wide", None),
        P("wide"),
    )
    out_specs = (P("wide", "narrow"), P("wide", None, "narrow"), P("wide", None, "narrow"))
    return jax.shard_map(body, mesh=mesh, in_specs=in_specs, out_specs=out_specs, check_vma=False)
```

profile of v0, /device:TPU:2, one launch (start us, length us, event | category | flops | bytes accessed | tf_op | source)
XLA Modules:
  0.0 689.3 jit_solution(3292197298421425880)
XLA Ops:
  7.2 1.0 copy.120
  8.2 1.1 copy.121
  9.9 1.2 dynamic_slice.6
  13.8 1.1 fusion.39
  14.9 1.0 fusion.30
  15.9 1.4 gather_fusion.1
  23.1 37.7 %all_gather.18 = bf16[256,8,128]{2,0,1:T(8,128)(2,1)S(1)} all-gather(bf16[8,8,128]{2,0,1:T(8,128)(2,1)S(1)} %copy.59), channel_id=1, replica_groups=mesh['wide'=32,'narrow'=16] {'wide'}, dimensions={0}, use_global_device_ids=true | all-gather | bytes 540672 | tf_op jit(solution)/shard_map/all_gather | solution.py:83
  60.8 28.5 %all_gather.20 = bf16[256,8,128]{2,0,1:T(8,128)(2,1)S(1)} all-gather(bf16[8,8,128]{2,0,1:T(8,128)(2,1)S(1)} %copy.60), channel_id=1, replica_groups=mesh['wide'=32,'narrow'=16] {'wide'}, dimensions={0}, use_global_device_ids=true | all-gather | bytes 540672 | tf_op jit(solution)/shard_map/all_gather | solution.py:82
  89.3 30.0 %all_gather.19 = bf16[2048,128]{1,0:T(8,128)(2,1)S(1)} all-gather(bf16[64,128]{1,0:T(8,128)(2,1)S(1)} %copy-done.7), channel_id=1, replica_groups=mesh['wide'=32,'narrow'=16] {'wide'}, dimensions={0}, use_global_device_ids=true | all-gather | bytes 540672 | tf_op jit(solution)/shard_map/all_gather | solution.py:78
  119.2 28.5 %all_gather.21 = bf16[2048,128]{1,0:T(8,128)(2,1)S(1)} all-gather(bf16[64,128]{1,0:T(8,128)(2,1)S(1)} %copy-done.8), channel_id=1, replica_groups=mesh['wide'=32,'narrow'=16] {'wide'}, dimensions={0}, use_global_device_ids=true | all-gather | bytes 540672 | tf_op jit(solution)/shard_map/all_gather | solution.py:79
  150.2 29.9 %all_gather.22 = bf16[2048,128]{1,0:T(8,128)(2,1)S(1)} all-gather(bf16[64,128]{1,0:T(8,128)(2,1)S(1)} %copy-done.9), channel_id=1, replica_groups=mesh['wide'=32,'narrow'=16] {'wide'}, dimensions={0}, use_global_device_ids=true | all-gather | bytes 540672 | tf_op jit(solution)/shard_map/all_gather | solution.py:80
  180.4 28.5 %all_gather.23 = bf16[2048,128]{1,0:T(8,128)(2,1)S(1)} all-gather(bf16[64,128]{1,0:T(8,128)(2,1)S(1)} %copy-done.10), channel_id=1, replica_groups=mesh['wide'=32,'narrow'=16] {'wide'}, dimensions={0}, use_global_device_ids=true | all-gather | bytes 540672 | tf_op jit(solution)/shard_map/all_gather | solution.py:81
  209.1 1.3 fusion.35
  210.9 1.2 reduce-window.6
  212.5 110.2 %all-reduce.3.cloned.1.call-done = f32[64,2048]{1,0:T(8,128)} async-done(((f32[64,2048]{1,0:T(8,128)}), f32[64,2048]{1,0:T(8,128)}) %all-reduce.3.cloned.1.call-update) | async-done | bytes 524304 | tf_op jit(solution)/shard_map/psum | solution.py:163
  322.8 1.2 fusion.36
  324.7 4.5 scatter_custom_fusion
  329.2 2.8 reshape.738
  332.0 4.8 copy.67
  336.9 125.1 %all_to_all.10 = bf16[32,2,9,2048]{3,1,2,0:T(2,128)(2,1)S(1)} all-to-all(bf16[32,2,9,2048]{3,1,2,0:T(2,128)(2,1)S(1)} %copy.67), channel_id=1, replica_groups=mesh['wide'=32,'narrow'=16] {'wide'}, dimensions={0} | all-to-all | bytes 4718592 | tf_op jit(solution)/shard_map/all_to_all | solution.py:184
  462.0 1.6 fusion.9
  463.6 4.1 fusion.1
  467.6 5.5 copy.70
  473.1 4.1 all-to-all-start.1
  477.5 1.2 fusion.127
  479.3 110.6 %all-to-all-done.1 = bf16[32,2,9,2048]{3,1,2,0:T(2,128)(2,1)S(1)} async-done(((bf16[32,2,9,2048]{3,1,2,0:T(2,128)(2,1)}), bf16[32,2,9,2048]{3,1,2,0:T(2,128)(2,1)S(1)}, u32[]{:S(2)}, u32[]{:S(2)}) %all-to-all-start.1) | async-done | bytes 2359328 | tf_op jit(solution)/shard_map/all_to_all | solution.py:191
  589.9 3.3 copy.71
  593.2 3.4 reshape.739
  596.6 3.3 gather_fusion
  599.9 4.2 fusion
  606.9 74.2 %reduce-scatter.2.cloned.1.call-done = f32[64,128]{1,0:T(8,128)} async-done(((f32[64,2048]{1,0:T(8,128)}), f32[64,128]{1,0:T(8,128)}) %reduce-scatter.2.cloned.1.call-update) | async-done | bytes 32784 | tf_op jit(solution)/shard_map/reduce_scatter | solution.py:196
  681.1 1.4 add_convert_fusion
  (104 shorter events, 13.8 us)
Async XLA Ops:
  7.2 456.4 %copy-start = (bf16[2,64,2048]{2,1,0:T(8,128)(2,1)S(1)}, bf16[2,64,2048]{2,1,0:T(8,128)(2,1)}, u32[]{:S(2)}) copy-start(bf16[2,64,2048]{2,1,0:T(8,128)(2,1)} %param.34) | copy-start | bytes 1572868
  7.2 315.6 %all-reduce.3.cloned.1.call-start = ((), (), s32[]{:S(2)}) async-start(), calls=%async_computation.3 | async-start | bytes 1048576 | tf_op jit(solution)/shard_map/psum | solution.py:163
  8.2 140.2 %copy-start.2 = (bf16[1,1024,128]{2,1,0:T(8,128)(2,1)}, bf16[1,1024,128]{2,1,0:T(8,128)(2,1)S(1)}, u32[]{:S(2)}) copy-start(bf16[1,1024,128]{2,1,0:T(8,128)(2,1)S(1)} %copy.120) | copy-start | bytes 786436
  8.2 14.8 %copy-start.12 = (bf16[8,8,128]{2,1,0:T(8,128)(2,1)S(1)}, bf16[8,8,128]{2,1,0:T(8,128)(2,1)}, u32[]{:S(2)}) copy-start(bf16[8,8,128]{2,1,0:T(8,128)(2,1)} %param.35) | copy-start | bytes 49156
  8.2 14.8 %copy-start.13 = (bf16[8,8,128]{2,1,0:T(8,128)(2,1)S(1)}, bf16[8,8,128]{2,1,0:T(8,128)(2,1)}, u32[]{:S(2)}) copy-start(bf16[8,8,128]{2,1,0:T(8,128)(2,1)} %param.36) | copy-start | bytes 49156
  15.9 73.4 %copy-start.7 = (bf16[64,128]{1,0:T(8,128)(2,1)S(1)}, bf16[64,128]{1,0:T(8,128)(2,1)}, u32[]{:S(2)}) copy-start(bf16[64,128]{1,0:T(8,128)(2,1)} %param.27) | copy-start | bytes 49156
  18.0 101.2 %copy-start.8 = (bf16[64,128]{1,0:T(8,128)(2,1)S(1)}, bf16[64,128]{1,0:T(8,128)(2,1)}, u32[]{:S(2)}) copy-start(bf16[64,128]{1,0:T(8,128)(2,1)} %param.28) | copy-start | bytes 49156
  18.8 128.9 %copy-start.6 = (bf16[64,2048]{1,0:T(8,128)(2,1)S(1)}, bf16[64,2048]{1,0:T(8,128)(2,1)}, u32[]{:S(2)}) copy-start(bf16[64,2048]{1,0:T(8,128)(2,1)} %param.24) | copy-start | bytes 786436
  18.8 128.9 %copy-start.16 = (f32[2048]{0:T(1024)S(1)}, f32[2048]{0:T(1024)}, u32[]{:S(2)}) copy-start(f32[2048]{0:T(1024)} %param.25) | copy-start | bytes 24580
  89.3 61.0 %copy-start.9 = (bf16[64,128]{1,0:T(8,128)(2,1)S(1)}, bf16[64,128]{1,0:T(8,128)(2,1)}, u32[]{:S(2)}) copy-start(bf16[64,128]{1,0:T(8,128)(2,1)} %param.29) | copy-start | bytes 49156
  147.7 32.6 %copy-start.10 = (bf16[64,128]{1,0:T(8,128)(2,1)S(1)}, bf16[64,128]{1,0:T(8,128)(2,1)}, u32[]{:S(2)}) copy-start(bf16[64,128]{1,0:T(8,128)(2,1)} %param.30) | copy-start | bytes 49156
  149.3 61.1 %copy-start.11 = (s32[64,8]{0,1:T(8,128)S(1)}, s32[64,8]{0,1:T(8,128)}, u32[]{:S(2)}) copy-start(s32[64,8]{0,1:T(8,128)} %param.42) | copy-start | bytes 6148
  180.4 143.6 %copy-start.14 = (f32[2048]{0:T(1024)S(1)}, f32[2048]{0:T(1024)}, u32[]{:S(2)}) copy-start(f32[2048]{0:T(1024)} %param.26) | copy-start | bytes 24580
  324.0 0.7 copy-start.5
  336.8 125.2 %copy-start.15 = (bf16[2,2048,64]{1,2,0:T(8,128)(2,1)S(1)}, bf16[2,2048,64]{1,2,0:T(8,128)(2,1)}, u32[]{:S(2)}) copy-start(bf16[2,2048,64]{1,2,0:T(8,128)(2,1)} %param.32) | copy-start | bytes 1572868
  473.1 116.7 %all-to-all-start.1 = ((bf16[32,2,9,2048]{3,1,2,0:T(2,128)(2,1)}), bf16[32,2,9,2048]{3,1,2,0:T(2,128)(2,1)S(1)}, u32[]{:S(2)}, u32[]{:S(2)}) async-start(bf16[32,2,9,2048]{3,1,2,0:T(2,128)(2,1)} %copy.70), calls=%async_computation.1 | async-start | bytes 4718592 | tf_op jit(solution)/shard_map/all_to_all | solution.py:191
  477.2 203.9 %reduce-scatter.2.cloned.1.call-start = ((), (), s32[]{:S(2)}) async-start(), calls=%async_computation.4 | async-start | bytes 557056 | tf_op jit(solution)/shard_map/reduce_scatter | solution.py:196
  599.9 5.1 copy-start.3
  606.0 76.5 %copy-start.4 = (bf16[1024,128]{1,0:T(8,128)(2,1)}, bf16[1024,128]{1,0:T(8,128)(2,1)S(1)}, u32[]{:S(2)}) copy-start(bf16[1024,128]{1,0:T(8,128)(2,1)S(1)} %scatter_fusion) | copy-start | bytes 786436
  606.9 75.6 %copy-start.1 = (bf16[1024,128]{1,0:T(8,128)(2,1)}, bf16[1024,128]{1,0:T(8,128)(2,1)S(1)}, u32[]{:S(2)}) copy-start(bf16[1024,128]{1,0:T(8,128)(2,1)S(1)} %scatter_fusion.1) | copy-start | bytes 786436
Sparse Core Ops, SparseCore 0:
  210.5 112.1 all-reduce.2
  604.3 76.7 reduce-scatter.1
where the time goes:
time: 690 us; the launch traced here: 689 us
  blocking collectives  308 us (45%)
  waiting for transfers between devices  295 us (43%)
  local copies, waits for them, and re-layouts  39.5 us (6%)
  between operations  17.8 us (3%)
  other arithmetic  12.3 us (2%)
  matrix products  12.3 us (2%)
    all_to_all x1, blocking collectives, body(): lax.all_to_all(send_rows, 'wide', split_axis=0, concat_axis=0, tiled=True)  125 us
    all_to_all x1, waiting for transfers between devices, body(): lax.all_to_all(produced, 'wide', split_axis=0, concat_axis=0, tiled=True)  111 us
    psum x1, waiting for transfers between devices, body(): summed = lax.psum(partial_value, 'narrow')  110 us
    reduce_scatter x1, waiting for transfers between devices, body(): lax.psum_scatter(partial_moe, 'narrow', scatter_dimension=1, tiled=True)  74.2 us
    all_gather x1, blocking collectives, body(): lax.all_gather(prefix_values, 'wide', axis=0, tiled=True)  37.7 us
    all_gather x1, blocking collectives, body(): lax.all_gather(query_weight, 'wide', axis=0, tiled=True)  30 us
    all_gather x1, blocking collectives, body(): lax.all_gather(value_weight, 'wide', axis=0, tiled=True)  29.9 us
    all_gather x1, blocking collectives, body(): lax.all_gather(output_weight, 'wide', axis=0, tiled=True)  28.5 us
  transfers between devices with their start and end apart: 3, of which 3 were waited for; matrix products, arithmetic and copies ran while one was open for 1% of the time, Pallas kernels for 0%

commit v1 on v0

--- a/solution.py
+++ b/solution.py
@@ -160,7 +160,9 @@
     partial_value = lax.dot_general(
         attended, output_full, (((1,), (1,)), ((), ())), preferred_element_type=jnp.float32
     )
-    summed = lax.psum(partial_value, "narrow")
+    summed = partial_value
+    for hop in (1, 2, 4, 8):
+        summed = summed + lax.ppermute(summed, "narrow", [(dev, dev ^ hop) for dev in range(16)])
     mixed = (hidden.astype(jnp.float32) + summed).astype(jnp.bfloat16)
     mixed_part = lax.dynamic_slice_in_dim(mixed, narrow_pos * slice_width, slice_width, 1)
     normed_moe = rms_scale(mixed, expert_gain)

time: 690 us -> 635 us (0.920)
  waiting for transfers between devices: 295 us -> 231 us
  starting transfers between devices: 4.36 us -> 19.4 us
    psum x1 -> x0, waiting for transfers between devices: 110 us -> none  [body(): summed = lax.psum(partial_value, 'narrow')]
    ppermute x0 -> x4, waiting for transfers between devices: none -> 44.9 us  [body(): lax.ppermute(summed, 'narrow', [(dev, dev ^ hop) for dev in range(16)])]
    ppermute x0 -> x4, starting transfers between devices: none -> 15 us  [body(): lax.ppermute(summed, 'narrow', [(dev, dev ^ hop) for dev in range(16)])]
  transfers between devices with their start and end apart: 3 -> 6, of which waited for: 3 -> 6; matrix products, arithmetic and copies ran while one was open for 1% -> 1% of each run, Pallas kernels for 0% -> 0%
where the time goes in v1:
time: 635 us; the launch traced here: 634 us
  blocking collectives  303 us (48%)
  waiting for transfers between devices  231 us (36%)
  local copies, waits for them, and re-layouts  39.5 us (6%)
  starting transfers between devices  19.4 us (3%)
  between operations  17.8 us (3%)
  matrix products  11.5 us (2%)
  other arithmetic  11.4 us (2%)
    all_to_all x1, blocking collectives, body(): lax.all_to_all(send_rows, 'wide', split_axis=0, concat_axis=0, tiled=True)  120 us
    all_to_all x1, waiting for transfers between devices, body(): lax.all_to_all(produced, 'wide', split_axis=0, concat_axis=0, tiled=True)  111 us
    reduce_scatter x1, waiting for transfers between devices, body(): lax.psum_scatter(partial_moe, 'narrow', scatter_dimension=1, tiled=True)  75.9 us
    ppermute x4, waiting for transfers between devices, body(): lax.ppermute(summed, 'narrow', [(dev, dev ^ hop) for dev in range(16)])  44.9 us
    all_gather x1, blocking collectives, body(): lax.all_gather(prefix_values, 'wide', axis=0, tiled=True)  37.7 us
    all_gather x1, blocking collectives, body(): lax.all_gather(query_weight, 'wide', axis=0, tiled=True)  30 us
    all_gather x1, blocking collectives, body(): lax.all_gather(value_weight, 'wide', axis=0, tiled=True)  29.9 us
    all_gather x1, blocking collectives, body(): lax.all_gather(output_weight, 'wide', axis=0, tiled=True)  28.5 us
  transfers between devices with their start and end apart: 6, of which 6 were waited for; matrix products, arithmetic and copies ran while one was open for 1% of the time, Pallas kernels for 0%

profile of v1, /device:TPU:2, one launch (start us, length us, event | category | flops | bytes accessed | tf_op | source)
XLA Modules:
  0.0 634.2 jit_solution(5509530451766584498)
XLA Ops:
  9.9 1.2 dynamic_slice.6
  15.9 1.4 gather_fusion.1
  23.1 37.7 %all_gather.18 = bf16[256,8,128]{2,0,1:T(8,128)(2,1)S(1)} all-gather(bf16[8,8,128]{2,0,1:T(8,128)(2,1)S(1)} %copy.59), channel_id=1, replica_groups=mesh['wide'=32,'narrow'=16] {'wide'}, dimensions={0}, use_global_device_ids=true | all-gather | bytes 540672 | tf_op jit(solution)/shard_map/all_gather | solution.py:83
  60.7 28.5 %all_gather.20 = bf16[256,8,128]{2,0,1:T(8,128)(2,1)S(1)} all-gather(bf16[8,8,128]{2,0,1:T(8,128)(2,1)S(1)} %copy.60), channel_id=1, replica_groups=mesh['wide'=32,'narrow'=16] {'wide'}, dimensions={0}, use_global_device_ids=true | all-gather | bytes 540672 | tf_op jit(solution)/shard_map/all_gather | solution.py:82
  89.2 30.0 %all_gather.19 = bf16[2048,128]{1,0:T(8,128)(2,1)S(1)} all-gather(bf16[64,128]{1,0:T(8,128)(2,1)S(1)} %copy-done.7), channel_id=1, replica_groups=mesh['wide'=32,'narrow'=16] {'wide'}, dimensions={0}, use_global_device_ids=true | all-gather | bytes 540672 | tf_op jit(solution)/shard_map/all_gather | solution.py:78
  119.2 28.5 %all_gather.21 = bf16[2048,128]{1,0:T(8,128)(2,1)S(1)} all-gather(bf16[64,128]{1,0:T(8,128)(2,1)S(1)} %copy-done.8), channel_id=1, replica_groups=mesh['wide'=32,'narrow'=16] {'wide'}, dimensions={0}, use_global_device_ids=true | all-gather | bytes 540672 | tf_op jit(solution)/shard_map/all_gather | solution.py:79
  150.2 29.9 %all_gather.22 = bf16[2048,128]{1,0:T(8,128)(2,1)S(1)} all-gather(bf16[64,128]{1,0:T(8,128)(2,1)S(1)} %copy-done.9), channel_id=1, replica_groups=mesh['wide'=32,'narrow'=16] {'wide'}, dimensions={0}, use_global_device_ids=true | all-gather | bytes 540672 | tf_op jit(solution)/shard_map/all_gather | solution.py:80
  180.3 28.5 %all_gather.23 = bf16[2048,128]{1,0:T(8,128)(2,1)S(1)} all-gather(bf16[64,128]{1,0:T(8,128)(2,1)S(1)} %copy-done.10), channel_id=1, replica_groups=mesh['wide'=32,'narrow'=16] {'wide'}, dimensions={0}, use_global_device_ids=true | all-gather | bytes 540672 | tf_op jit(solution)/shard_map/all_gather | solution.py:81
  209.6 2.4 collective-permute-start
  212.0 13.6 %collective-permute-done = f32[64,2048]{1,0:T(8,128)S(1)} collective-permute-done((f32[64,2048]{1,0:T(8,128)S(1)}, f32[64,2048]{1,0:T(8,128)S(1)}, u32[]{:S(2)}, u32[]{:S(2)}) %collective-permute-start) | collective-permute-done | bytes 524320 | tf_op jit(solution)/shard_map/ppermute | solution.py:165
  225.7 4.0 collective-permute-start.1
  229.7 12.7 %collective-permute-done.1 = f32[64,2048]{1,0:T(8,128)S(1)} collective-permute-done((f32[64,2048]{1,0:T(8,128)S(1)}, f32[64,2048]{1,0:T(8,128)S(1)}, u32[]{:S(2)}, u32[]{:S(2)}) %collective-permute-start.1) | collective-permute-done | bytes 524320 | tf_op jit(solution)/shard_map/ppermute | solution.py:165
  242.5 3.5 collective-permute-start.2
  246.2 10.7 %collective-permute-done.2 = f32[64,2048]{1,0:T(8,128)S(1)} collective-permute-done((f32[64,2048]{1,0:T(8,128)S(1)}, f32[64,2048]{1,0:T(8,128)S(1)}, u32[]{:S(2)}, u32[]{:S(2)}) %collective-permute-start.2) | collective-permute-done | bytes 524320 | tf_op jit(solution)/shard_map/ppermute | solution.py:165
  256.9 5.1 collective-permute-start.3
  262.3 1.2 reduce-window.6
  264.0 7.9 %collective-permute-done.3 = f32[64,2048]{1,0:T(8,128)S(1)} collective-permute-done((f32[64,2048]{1,0:T(8,128)S(1)}, f32[64,2048]{1,0:T(8,128)S(1)}, u32[]{:S(2)}, u32[]{:S(2)}) %collective-permute-start.3) | collective-permute-done | bytes 524320 | tf_op jit(solution)/shard_map/ppermute | solution.py:165
  272.8 4.5 scatter_custom_fusion
  277.3 2.8 reshape.738
  280.1 4.8 copy.67
  284.9 120.2 %all_to_all.10 = bf16[32,2,9,2048]{3,1,2,0:T(2,128)(2,1)S(1)} all-to-all(bf16[32,2,9,2048]{3,1,2,0:T(2,128)(2,1)S(1)} %copy.67), channel_id=1, replica_groups=mesh['wide'=32,'narrow'=16] {'wide'}, dimensions={0} | all-to-all | bytes 4718592 | tf_op jit(solution)/shard_map/all_to_all | solution.py:186
  405.2 1.6 fusion.9
  406.7 4.1 fusion.1
  410.8 5.5 copy.70
  416.3 4.1 all-to-all-start.1
  422.4 110.6 %all-to-all-done.1 = bf16[32,2,9,2048]{3,1,2,0:T(2,128)(2,1)S(1)} async-done(((bf16[32,2,9,2048]{3,1,2,0:T(2,128)(2,1)}), bf16[32,2,9,2048]{3,1,2,0:T(2,128)(2,1)S(1)}, u32[]{:S(2)}, u32[]{:S(2)}) %all-to-all-start.1) | async-done | bytes 2359328 | tf_op jit(solution)/shard_map/all_to_all | solution.py:193
  533.0 3.3 copy.71
  536.3 3.4 reshape.739
  539.7 3.3 gather_fusion
  543.1 4.2 fusion
  550.1 75.9 %reduce-scatter.2.cloned.1.call-done = f32[64,128]{1,0:T(8,128)} async-done(((f32[64,2048]{1,0:T(8,128)}), f32[64,128]{1,0:T(8,128)}) %reduce-scatter.2.cloned.1.call-update) | async-done | bytes 32784 | tf_op jit(solution)/shard_map/reduce_scatter | solution.py:198
  626.0 1.4 add_convert_fusion
  (112 shorter events, 19.9 us)
Async XLA Ops:
  7.2 399.6 %copy-start = (bf16[2,64,2048]{2,1,0:T(8,128)(2,1)S(1)}, bf16[2,64,2048]{2,1,0:T(8,128)(2,1)}, u32[]{:S(2)}) copy-start(bf16[2,64,2048]{2,1,0:T(8,128)(2,1)} %param.34) | copy-start | bytes 1572868
  8.2 140.2 %copy-start.2 = (bf16[1,1024,128]{2,1,0:T(8,128)(2,1)}, bf16[1,1024,128]{2,1,0:T(8,128)(2,1)S(1)}, u32[]{:S(2)}) copy-start(bf16[1,1024,128]{2,1,0:T(8,128)(2,1)S(1)} %copy.119) | copy-start | bytes 786436
  8.2 14.8 %copy-start.12 = (bf16[8,8,128]{2,1,0:T(8,128)(2,1)S(1)}, bf16[8,8,128]{2,1,0:T(8,128)(2,1)}, u32[]{:S(2)}) copy-start(bf16[8,8,128]{2,1,0:T(8,128)(2,1)} %param.35) | copy-start | bytes 49156
  8.2 14.8 %copy-start.13 = (bf16[8,8,128]{2,1,0:T(8,128)(2,1)S(1)}, bf16[8,8,128]{2,1,0:T(8,128)(2,1)}, u32[]{:S(2)}) copy-start(bf16[8,8,128]{2,1,0:T(8,128)(2,1)} %param.36) | copy-start | bytes 49156
  15.9 73.4 %copy-start.7 = (bf16[64,128]{1,0:T(8,128)(2,1)S(1)}, bf16[64,128]{1,0:T(8,128)(2,1)}, u32[]{:S(2)}) copy-start(bf16[64,128]{1,0:T(8,128)(2,1)} %param.27) | copy-start | bytes 49156
  18.0 101.2 %copy-start.8 = (bf16[64,128]{1,0:T(8,128)(2,1)S(1)}, bf16[64,128]{1,0:T(8,128)(2,1)}, u32[]{:S(2)}) copy-start(bf16[64,128]{1,0:T(8,128)(2,1)} %param.28) | copy-start | bytes 49156
  18.8 128.9 %copy-start.6 = (bf16[64,2048]{1,0:T(8,128)(2,1)S(1)}, bf16[64,2048]{1,0:T(8,128)(2,1)}, u32[]{:S(2)}) copy-start(bf16[64,2048]{1,0:T(8,128)(2,1)} %param.24) | copy-start | bytes 786436
  18.8 128.9 %copy-start.16 = (f32[2048]{0:T(1024)S(1)}, f32[2048]{0:T(1024)}, u32[]{:S(2)}) copy-start(f32[2048]{0:T(1024)} %param.25) | copy-start | bytes 24580
  89.2 61.0 %copy-start.9 = (bf16[64,128]{1,0:T(8,128)(2,1)S(1)}, bf16[64,128]{1,0:T(8,128)(2,1)}, u32[]{:S(2)}) copy-start(bf16[64,128]{1,0:T(8,128)(2,1)} %param.29) | copy-start | bytes 49156
  147.7 32.6 %copy-start.10 = (bf16[64,128]{1,0:T(8,128)(2,1)S(1)}, bf16[64,128]{1,0:T(8,128)(2,1)}, u32[]{:S(2)}) copy-start(bf16[64,128]{1,0:T(8,128)(2,1)} %param.30) | copy-start | bytes 49156
  208.9 37.2 %copy-start.11 = (s32[64,8]{0,1:T(8,128)S(1)}, s32[64,8]{0,1:T(8,128)}, u32[]{:S(2)}) copy-start(s32[64,8]{0,1:T(8,128)} %param.42) | copy-start | bytes 6148
  209.6 16.1 %collective-permute-start = (f32[64,2048]{1,0:T(8,128)S(1)}, f32[64,2048]{1,0:T(8,128)S(1)}, u32[]{:S(2)}, u32[]{:S(2)}) collective-permute-start(f32[64,2048]{1,0:T(8,128)S(1)} %fusion.35), channel_id=1, source_target_pairs={{0,1},{1,0},{2,3},{3,2},{4,5},{5,4},{6,7},{7,6},{8,9},{9,8},{10,11... | collective-permute-start | bytes 1572872 | tf_op jit(solution)/shard_map/ppermute | solution.py:165
  225.7 16.8 %collective-permute-start.1 = (f32[64,2048]{1,0:T(8,128)S(1)}, f32[64,2048]{1,0:T(8,128)S(1)}, u32[]{:S(2)}, u32[]{:S(2)}) collective-permute-start(f32[64,2048]{1,0:T(8,128)S(1)} %add.165), channel_id=1, source_target_pairs={{0,2},{1,3},{2,0},{3,1},{4,6},{5,7},{6,4},{7,5},{8,10},{9,11},{10,... | collective-permute-start | bytes 1572872 | tf_op jit(solution)/shard_map/ppermute | solution.py:165
  242.5 29.6 %copy-start.14 = (f32[2048]{0:T(1024)S(1)}, f32[2048]{0:T(1024)}, u32[]{:S(2)}) copy-start(f32[2048]{0:T(1024)} %param.26) | copy-start | bytes 24580
  242.5 14.3 %collective-permute-start.2 = (f32[64,2048]{1,0:T(8,128)S(1)}, f32[64,2048]{1,0:T(8,128)S(1)}, u32[]{:S(2)}, u32[]{:S(2)}) collective-permute-start(f32[64,2048]{1,0:T(8,128)S(1)} %add.166), channel_id=1, source_target_pairs={{0,4},{1,5},{2,6},{3,7},{4,0},{5,1},{6,2},{7,3},{8,12},{9,13},{10,... | collective-permute-start | bytes 1572872 | tf_op jit(solution)/shard_map/ppermute | solution.py:165
  256.9 14.9 %collective-permute-start.3 = (f32[64,2048]{1,0:T(8,128)S(1)}, f32[64,2048]{1,0:T(8,128)S(1)}, u32[]{:S(2)}, u32[]{:S(2)}) collective-permute-start(f32[64,2048]{1,0:T(8,128)S(1)} %add.167), channel_id=1, source_target_pairs={{0,8},{1,9},{2,10},{3,11},{4,12},{5,13},{6,14},{7,15},{8,0},{9,1},... | collective-permute-start | bytes 1572872 | tf_op jit(solution)/shard_map/ppermute | solution.py:165
  272.1 0.7 copy-start.5
  284.9 120.2 %copy-start.15 = (bf16[2,2048,64]{1,2,0:T(8,128)(2,1)S(1)}, bf16[2,2048,64]{1,2,0:T(8,128)(2,1)}, u32[]{:S(2)}) copy-start(bf16[2,2048,64]{1,2,0:T(8,128)(2,1)} %param.32) | copy-start | bytes 1572868
  416.3 116.7 %all-to-all-start.1 = ((bf16[32,2,9,2048]{3,1,2,0:T(2,128)(2,1)}), bf16[32,2,9,2048]{3,1,2,0:T(2,128)(2,1)S(1)}, u32[]{:S(2)}, u32[]{:S(2)}) async-start(bf16[32,2,9,2048]{3,1,2,0:T(2,128)(2,1)} %copy.70), calls=%async_computation.1 | async-start | bytes 4718592 | tf_op jit(solution)/shard_map/all_to_all | solution.py:193
  420.3 205.7 %reduce-scatter.2.cloned.1.call-start = ((), (), s32[]{:S(2)}) async-start(), calls=%async_computation.3 | async-start | bytes 557056 | tf_op jit(solution)/shard_map/reduce_scatter | solution.py:198
  543.1 5.1 copy-start.3
  549.1 78.3 %copy-start.4 = (bf16[1024,128]{1,0:T(8,128)(2,1)}, bf16[1024,128]{1,0:T(8,128)(2,1)S(1)}, u32[]{:S(2)}) copy-start(bf16[1024,128]{1,0:T(8,128)(2,1)S(1)} %scatter_fusion) | copy-start | bytes 786436
  550.1 77.3 %copy-start.1 = (bf16[1024,128]{1,0:T(8,128)(2,1)}, bf16[1024,128]{1,0:T(8,128)(2,1)S(1)}, u32[]{:S(2)}) copy-start(bf16[1024,128]{1,0:T(8,128)(2,1)S(1)} %scatter_fusion.1) | copy-start | bytes 786436
Sparse Core Ops, SparseCore 0:
  547.5 78.5 reduce-scatter.1
